TPU v7x, 256 devices: a whole 4x4x8 slice. The times are simulated.
256 devices in a mesh: section: 8 (over z), dp: 32 (over x, y, core).
Axes of the slice: x: 4, y: 4, z: 8, core: 2. Of those that a mesh axis runs over, the one named last changes fastest.
Arguments:
- output_gradient: bfloat16 [8, 4096, 2048], P('section', 'dp'), may hold values from -6 to 6
- saved_input: bfloat16 [8, 4096, 8192], P('section', 'dp'), may hold values from -6 to 6
- frozen_matrix: bfloat16 [8, 8192, 2048], P('section', 'dp'), may hold values from -0.0625 to 0.0625
- adapter_down_maps: bfloat16 [8, 8192, 2048], P('section', None, 'dp'), may hold values from -0.0625 to 0.0625
- adapter_up_maps: bfloat16 [8, 2048, 2048], P('section', None, 'dp'), may hold values from -0.125 to 0.125
- token_tenants: int32 [8, 4096], P('section'), may hold values from 0 to 31, never falling along the last dimension, each value on 1 to 256 neighbouring positions
- tenant_slot_lookup: int32 [8, 32], P('section'), may hold values from 0 to 31, each once within a row
Outputs:
- passed_grad: bfloat16 [8, 4096, 8192], P('section', 'dp')
- down_gradient: bfloat16 [8, 8192, 2048], P('section', None, 'dp')
- up_gradient: bfloat16 [8, 2048, 2048], P('section', None, 'dp')
Inputs may be any that keep to these rules, and one draw needn't show every extreme that they name: `token_tenants`: within a section the ids never fall; each of the 32 tenants has 1 to 256 tokens, one exactly 256. `tenant_slot_lookup`: each section's row is a permutation.
All inputs are finite; a program needn't handle non-finite values.
Results may differ from a plain program's by a relative error of at most 0.005.
Values may be sent and summed in bfloat16 or wider, within the bound.
A program may use at most 128 MiB of HBM per device.

v0:
```python
import jax
import jax.numpy as jnp
from jax import lax
from jax.sharding import PartitionSpec as P

ADAPTER_RANK = 64
MOST = 256
adapter_scale = 2.0


def from_behind(value, axis, steps):
    count = lax.axis_size(axis)
    first, last = (max(0, -steps), min(count, count - steps))
    return lax.ppermute(value, axis, [(source, source + steps) for source in range(first, last)])


def block_layout(tenant_row, slot_table, tenants, most):
    tokens = tenant_row.shape[0]
    tenant_range = jnp.arange(tenants, dtype=jnp.int32)
    member = (tenant_range[:, None] == tenant_row[None, :]).astype(jnp.int32)
    counts = jnp.sum(member, axis=1)
    starts = jnp.cumsum(counts) - counts
    owner_match = (slot_table[None, :] == tenant_range[:, None]).astype(jnp.int32)
    slot_start = jnp.sum(owner_match * starts[None, :], axis=1)
    slot_count = jnp.sum(owner_match * counts[None, :], axis=1)
    place = jnp.arange(most, dtype=jnp.int32)
    live_slot = place[None, :] < slot_count[:, None]
    row_index = jnp.minimum(slot_start[:, None] + place[None, :], tokens - 1)
    token_slot = jnp.sum(member * slot_table[:, None], axis=0)
    token_start = jnp.sum(member * starts[:, None], axis=0)
    token_place = token_slot * most + jnp.arange(tokens, dtype=jnp.int32) - token_start
    return (row_index, live_slot, token_place)


def masked_rows(rows, row_index, live_slot):
    picked = rows[row_index]
    return jnp.where(live_slot[:, :, None], picked, jnp.zeros((), picked.dtype))


def adapter_term(rank_up_values, down_three, token_place):
    blocks = jnp.einsum(
        "kpr,dkr->kpd", rank_up_values, down_three, preferred_element_type=jnp.float32
    )
    return blocks.reshape(blocks.shape[0] * blocks.shape[1], blocks.shape[2])[token_place]


def local(
    output_gradient,
    saved_input,
    frozen_matrix,
    adapter_down_maps,
    adapter_up_maps,
    token_tenants,
    tenant_slot_lookup,
):
    grad_rows = output_gradient[0]
    saved_rows = saved_input[0]
    weight = frozen_matrix[0]
    local_width = weight.shape[0]
    out_width = weight.shape[1]
    kv_local = out_width // lax.axis_size("dp")
    kv_offset = lax.axis_index("dp") * kv_local
    tenants = tenant_slot_lookup.shape[1]
    contract_last = (((1,), (1,)), ((), ()))
    row_index, live_slot, token_place = block_layout(
        token_tenants[0], tenant_slot_lookup[0], tenants, MOST
    )
    saved_cols = lax.all_to_all(saved_rows, "dp", split_axis=1, concat_axis=0, tiled=True)
    saved_input_blocks = masked_rows(saved_cols, row_index, live_slot)
    block_rows = lax.all_gather(grad_rows, "dp", axis=0, tiled=True)
    frozen_part = lax.dot_general(
        block_rows, weight, contract_last, preferred_element_type=jnp.float32
    )
    own_cols = lax.dynamic_slice_in_dim(block_rows, kv_offset, kv_local, 1).astype(jnp.float32)
    joined = jnp.concatenate([frozen_part, own_cols], axis=1)
    frozen_product = joined[:, :local_width]
    grad_cols = joined[:, local_width:].astype(jnp.bfloat16)
    down_cols, up_cols = (
        lax.all_to_all(adapter_down_maps[0], "dp", split_axis=0, concat_axis=1, tiled=True),
        lax.all_to_all(adapter_up_maps[0], "dp", split_axis=0, concat_axis=1, tiled=True),
    )
    down_three = down_cols.reshape(local_width, tenants, ADAPTER_RANK)
    up_three = up_cols.reshape(kv_local, tenants, ADAPTER_RANK)
    gradient_blocks = masked_rows(grad_cols, row_index, live_slot)
    up_part = jnp.einsum(
        "kpe,ekr->kpr", gradient_blocks, up_three, preferred_element_type=jnp.float32
    )
    down_part = jnp.einsum(
        "kpd,dkr->kpr", saved_input_blocks, down_three, preferred_element_type=jnp.float32
    )
    up_total, down_total = lax.psum((up_part, down_part), "dp")
    rank_up_values = up_total.astype(jnp.bfloat16)
    rank_down_values = down_total.astype(jnp.bfloat16)
    adapter_slot = adapter_term(rank_up_values, down_three, token_place)
    down_grad_cols = (
        (
            adapter_scale
            * jnp.einsum(
                "tfv,tfy->vty",
                saved_input_blocks,
                rank_up_values,
                preferred_element_type=jnp.float32,
            )
        )
        .reshape(local_width, tenants * ADAPTER_RANK)
        .astype(jnp.bfloat16)
    )
    up_grad_cols = (
        (
            adapter_scale
            * jnp.einsum(
                "ohz,ohq->zoq",
                gradient_blocks,
                rank_down_values,
                preferred_element_type=jnp.float32,
            )
        )
        .reshape(kv_local, tenants * ADAPTER_RANK)
        .astype(jnp.bfloat16)
    )
    down_gradient, up_gradient = (
        lax.all_to_all(down_grad_cols, "dp", split_axis=1, concat_axis=0, tiled=True),
        lax.all_to_all(up_grad_cols, "dp", split_axis=1, concat_axis=0, tiled=True),
    )
    input_columns = (frozen_product + adapter_scale * adapter_slot).astype(jnp.bfloat16)
    input_rows = lax.all_to_all(input_columns, "dp", split_axis=0, concat_axis=1, tiled=True)
    passed = from_behind(input_rows, "section", -1)
    return (passed[None], down_gradient[None], up_gradient[None])


def solution(mesh):
    return jax.shard_map(
        local,
        mesh=mesh,
        in_specs=(
            P("section", "dp", None),
            P("section", "dp", None),
            P("section", "dp", None),
            P("section", None, "dp"),
            P("section", None, "dp"),
            P("section", None),
            P("section", None),
        ),
        out_specs=(P("section", "dp", None), P("section", None, "dp"), P("section", None, "dp")),
        check_vma=False,
    )
```

profile of v0, /device:TPU:1, one launch (start us, length us, event | category | flops | bytes accessed | tf_op | source)
XLA Modules:
  0.0 439.3 jit_solution(11001682472240546703)
XLA Ops:
  7.2 0.0 copy-start
  7.2 0.0 copy-start.2
  7.2 0.0 all-gather.3.cloned.1.call-start
  7.2 0.7 all-gather.3.cloned.1.call-update
  7.9 2.3 all_to_all.72
  10.2 2.0 copy.35
  12.2 2.1 reshape.196
  14.4 8.6 %all-to-all-start = ((bf16[32,2,2048]{2,1,0:T(2,128)(2,1)}), bf16[32,2,2048]{2,1,0:T(2,128)(2,1)S(1)}, u32[]{:S(2)}, u32[]{:S(2)}) async-start(bf16[32,2,2048]{2,1,0:T(2,128)(2,1)} %reshape.196), calls=%async_computation | async-start | bytes 524288 | tf_op jit(solution)/shard_map/all_to_all | solution.py:80
  23.0 0.0 copy-done.2
  23.0 0.6 copy.33
  23.6 0.0 copy-start.4
  23.6 0.0 copy-start.5
  23.6 2.5 copy.27
  26.1 6.0 %all-to-all-done = bf16[32,2,2048]{2,1,0:T(2,128)(2,1)S(1)} async-done(((bf16[32,2,2048]{2,1,0:T(2,128)(2,1)}), bf16[32,2,2048]{2,1,0:T(2,128)(2,1)S(1)}, u32[]{:S(2)}, u32[]{:S(2)}) %all-to-all-start) | async-done | bytes 262176 | tf_op jit(solution)/shard_map/all_to_all | solution.py:80
  32.1 3.8 all-to-all-start.3
  35.9 0.0 copy-done.4
  35.9 0.2 convert_reduce_fusion
  36.0 0.1 copy.22
  36.1 0.1 reduce-window.7
  36.2 0.1 reduce
  36.3 0.0 copy-done.5
  36.3 0.1 select_reduce_fusion.3
  36.4 0.1 fusion.26
  36.6 1.5 copy.32
  38.1 1.6 copy.25
  39.6 0.2 select_reduce_fusion.1
  39.8 0.1 iota_compare_fusion.1
  39.9 25.3 %all-to-all-done.3 = bf16[128,32,256]{2,0,1:T(8,128)(2,1)S(1)} async-done(((bf16[128,32,256]{2,0,1:T(8,128)(2,1)}), bf16[128,32,256]{2,0,1:T(8,128)(2,1)S(1)}, u32[]{:S(2)}, u32[]{:S(2)}) %all-to-all-start.3) | async-done | bytes 2097184 | tf_op jit(solution)/shard_map/all_to_all | solution.py:68
  65.2 5.5 %all-to-all-start.1 = ((bf16[32,256,64]{1,2,0:T(8,128)(2,1)}), bf16[32,256,64]{1,2,0:T(8,128)(2,1)}, u32[]{:S(2)}, u32[]{:S(2)}) async-start(bf16[32,256,64]{1,2,0:T(8,128)(2,1)} %copy.25), calls=%async_computation.1 | async-start | bytes 2097152 | tf_op jit(solution)/shard_map/all_to_all | solution.py:79
  70.8 1.2 reshape.197
  72.0 33.1 %gather_fusion.2 = bf16[8192,256]{1,0:T(8,128)(2,1)} fusion(bf16[4096,256]{1,0:T(8,128)(2,1)S(1)} %bitcast.79, s32[8192]{0:T(1024)S(1)} %broadcast_clamp_fusion), kind=kCustom, calls=%fused_computation.2 | custom fusion | bytes 8421376 | tf_op jit(solution)/shard_map/gather | solution.py:36
  105.1 0.0 all-to-all-done.1
  105.1 4.6 %fusion.8 = f32[32,256,64]{1,2,0:T(8,128)} fusion(bf16[32,256,256]{2,1,0:T(8,128)(2,1)} %bitcast.86, pred[32,256]{1,0:T(8,128)(4,1)S(1)} %iota_compare_fusion.1, bf16[32,256,64]{1,2,0:T(8,128)(2,1)} %all-to-all-done.1), kind=kOutput, calls=%fused_computation.8 | convolution fusion | flops 270532608 | bytes 7348224 | tf_op jit(solution)/shard_map/kpd,dkr->kpr/dot_general | solution.py:88
  109.7 12.3 %all-gather.3.cloned.1.call-done = bf16[1,4096,2048]{2,1,0:T(8,128)(2,1)} async-done(((bf16[1,128,2048]{2,1,0:T(8,128)(2,1)}), bf16[1,4096,2048]{2,1,0:T(8,128)(2,1)}) %all-gather.3.cloned.1.call-update) | async-done | bytes 16777232 | tf_op jit(solution)/shard_map/all_gather | solution.py:70
  122.0 1.6 dynamic-slice_bitcast_fusion
  123.5 29.5 %gather_fusion = bf16[8192,64]{1,0:T(8,128)(2,1)} fusion(bf16[4096,64]{1,0:T(8,128)(2,1)S(1)} %dynamic-slice_bitcast_fusion, s32[8192]{0:T(1024)S(1)} %broadcast_clamp_fusion), kind=kCustom, calls=%fused_computation | custom fusion | bytes 2129920 | tf_op jit(solution)/shard_map/gather | solution.py:36
  153.0 2.7 copy.23
  155.7 1.8 fusion.20
  157.5 146.1 %all-reduce.2 = (bf16[32,256,64]{1,2,0:T(8,128)(2,1)}, bf16[32,256,64]{1,2,0:T(8,128)(2,1)}) all-reduce(f32[32,256,64]{1,2,0:T(8,128)S(1)} %fusion.20, f32[32,256,64]{1,2,0:T(8,128)} %fusion.8), channel_id=1, replica_groups=mesh['section'=8,'dp'=32] {'dp'}, use_global_device_ids=true, to_apply=%region_4.5 | all-reduce | flops 1048576 | bytes 6291456 | tf_op jit(solution)/shard_map/psum | solution.py:91
  303.6 6.1 %fusion.16 = f32[32,256,256]{2,1,0:T(8,128)} fusion(bf16[32,256,64]{1,2,0:T(8,128)(2,1)} %all-to-all-done.1, bf16[32,256,64]{1,2,0:T(8,128)(2,1)} %get-tuple-element.7), kind=kOutput, calls=%fused_computation.18 | convolution fusion | flops 268435456 | bytes 10485760 | tf_op jit(solution)/shard_map/kpr,dkr->kpd/dot_general | solution.py:41
  309.7 19.5 %gather_fusion.1 = f32[4096,256]{1,0:T(8,128)} fusion(f32[8192,256]{1,0:T(8,128)} %bitcast.80, s32[4096]{0:T(1024)S(1)} %broadcast_clamp_fusion.1), kind=kCustom, calls=%fused_computation.1 | custom fusion | bytes 8404992 | tf_op jit(solution)/shard_map/gather | solution.py:44
  329.2 0.0 copy-done
  329.2 11.8 %fusion.5 = bf16[4096,256]{1,0:T(8,128)(2,1)S(1)} fusion(bf16[1,4096,2048]{2,1,0:T(8,128)(2,1)} %all-gather.3.cloned.1.call-done, f32[4096,256]{1,0:T(8,128)} %gather_fusion.1, bf16[1,256,2048]{2,1,0:T(8,128)(2,1)S(1)} %copy-done), kind=kOutput, calls=%fused_computation.6 | convolution fusion | flops 4298113024 | bytes 24117248 | tf_op jit(solution)/shard_map/dot_general | solution.py:71
  341.0 0.0 copy-start.1
  341.1 0.0 copy-start.6
  341.1 37.0 %all_to_all.96 = bf16[32,128,256]{2,1,0:T(8,128)(2,1)S(1)} all-to-all(bf16[32,128,256]{2,1,0:T(8,128)(2,1)S(1)} %bitcast.89), channel_id=1, replica_groups=mesh['section'=8,'dp'=32] {'dp'}, dimensions={0} | all-to-all | bytes 4194304 | tf_op jit(solution)/shard_map/all_to_all | solution.py:126
  378.1 1.5 copy.30
  379.6 1.3 collective-permute-start
  380.9 0.0 copy-done.1
  380.9 0.4 fusion.31
  381.4 1.1 reshape.198
  382.5 3.9 all-to-all-start.5
  386.4 0.0 copy-done.3
  386.4 4.8 %fusion.12 = bf16[256,32,64]{0,2,1:T(8,128)(2,1)} fusion(bf16[32,256,256]{2,1,0:T(8,128)(2,1)} %bitcast.87, pred[32,256]{1,0:T(8,128)(4,1)S(1)} %iota_compare_fusion.1, bf16[32,256,64]{1,2,0:T(8,128)(2,1)S(1)} %copy-done.3), kind=kOutput, calls=%fused_computation.13 | convolution fusion | flops 271581184 | bytes 6299648 | tf_op jit(solution)/shard_map/tfv,tfy->vty/dot_general | solution.py:98
  391.2 4.2 all-to-all-done.5
  395.4 3.8 all-to-all-start.4
  399.2 0.4 reshape.199
  399.6 0.3 copy.29
  399.9 1.2 broadcast_in_dim.53
  401.1 15.1 %all-to-all-done.4 = bf16[256,32,64]{0,2,1:T(8,128)(2,1)S(1)} async-done(((bf16[256,32,64]{0,2,1:T(8,128)(2,1)}), bf16[256,32,64]{0,2,1:T(8,128)(2,1)S(1)}, u32[]{:S(2)}, u32[]{:S(2)}) %all-to-all-start.4) | async-done | bytes 1048608 | tf_op jit(solution)/shard_map/all_to_all | solution.py:122
  416.2 0.6 copy.28
  416.8 1.3 broadcast_in_dim.52
  418.1 11.3 %collective-permute-done = bf16[128,8192]{1,0:T(8,128)(2,1)} collective-permute-done((bf16[128,8192]{1,0:T(8,128)(2,1)}, bf16[128,8192]{1,0:T(8,128)(2,1)}, u32[]{:S(2)}, u32[]{:S(2)}) %collective-permute-start) | collective-permute-done | bytes 2097184 | tf_op jit(solution)/shard_map/ppermute | solution.py:14
  429.4 3.1 copy.41
  (9 shorter events, 0.1 us)
Async XLA Ops:
  7.2 322.1 %copy-start = (bf16[1,256,2048]{2,1,0:T(8,128)(2,1)S(1)}, bf16[1,256,2048]{2,1,0:T(8,128)(2,1)}, u32[]{:S(2)}) copy-start(bf16[1,256,2048]{2,1,0:T(8,128)(2,1)} %param.9) | copy-start | bytes 3145732
  7.2 15.8 %copy-start.2 = (bf16[1,128,8192]{2,1,0:T(8,128)(2,1)S(1)}, bf16[1,128,8192]{2,1,0:T(8,128)(2,1)}, u32[]{:S(2)}) copy-start(bf16[1,128,8192]{2,1,0:T(8,128)(2,1)} %param.8) | copy-start | bytes 6291460
  7.2 114.8 %all-gather.3.cloned.1.call-start = ((), (), s32[]{:S(2)}) async-start(), calls=%async_computation.6 | async-start | bytes 17301504 | tf_op jit(solution)/shard_map/all_gather | solution.py:70
  14.4 17.7 %all-to-all-start = ((bf16[32,2,2048]{2,1,0:T(2,128)(2,1)}), bf16[32,2,2048]{2,1,0:T(2,128)(2,1)S(1)}, u32[]{:S(2)}, u32[]{:S(2)}) async-start(bf16[32,2,2048]{2,1,0:T(2,128)(2,1)} %reshape.196), calls=%async_computation | async-start | bytes 524288 | tf_op jit(solution)/shard_map/all_to_all | solution.py:80
  23.6 12.3 %copy-start.4 = (s32[1,4096]{1,0:T(1,128)S(1)}, s32[1,4096]{1,0:T(1,128)}, u32[]{:S(2)}) copy-start(s32[1,4096]{1,0:T(1,128)} %param.12) | copy-start | bytes 49156
  23.6 12.7 %copy-start.5 = (s32[1,32]{1,0:T(1,128)S(1)}, s32[1,32]{1,0:T(1,128)}, u32[]{:S(2)}) copy-start(s32[1,32]{1,0:T(1,128)} %param.13) | copy-start | bytes 388
  32.1 33.2 %all-to-all-start.3 = ((bf16[128,32,256]{2,0,1:T(8,128)(2,1)}), bf16[128,32,256]{2,0,1:T(8,128)(2,1)S(1)}, u32[]{:S(2)}, u32[]{:S(2)}) async-start(bf16[128,32,256]{2,0,1:T(8,128)(2,1)} %copy.27), calls=%async_computation.3 | async-start | bytes 4194304 | tf_op jit(solution)/shard_map/all_to_all | solution.py:68
  65.2 39.9 %all-to-all-start.1 = ((bf16[32,256,64]{1,2,0:T(8,128)(2,1)}), bf16[32,256,64]{1,2,0:T(8,128)(2,1)}, u32[]{:S(2)}, u32[]{:S(2)}) async-start(bf16[32,256,64]{1,2,0:T(8,128)(2,1)} %copy.25), calls=%async_computation.1 | async-start | bytes 2097152 | tf_op jit(solution)/shard_map/all_to_all | solution.py:79
  341.0 39.9 %copy-start.1 = (bf16[32,256,64]{1,2,0:T(8,128)(2,1)S(1)}, bf16[32,256,64]{1,2,0:T(8,128)(2,1)}, u32[]{:S(2)}) copy-start(bf16[32,256,64]{1,2,0:T(8,128)(2,1)} %copy.23) | copy-start | bytes 3145732
  341.1 39.9 %copy-start.6 = (bf16[32,256,64]{1,2,0:T(8,128)(2,1)S(1)}, bf16[32,256,64]{1,2,0:T(8,128)(2,1)}, u32[]{:S(2)}) copy-start(bf16[32,256,64]{1,2,0:T(8,128)(2,1)} %get-tuple-element.8) | copy-start | bytes 3145732
  378.1 8.3 %copy-start.3 = (bf16[32,256,64]{1,2,0:T(8,128)(2,1)S(1)}, bf16[32,256,64]{1,2,0:T(8,128)(2,1)}, u32[]{:S(2)}) copy-start(bf16[32,256,64]{1,2,0:T(8,128)(2,1)} %get-tuple-element.7) | copy-start | bytes 3145732
  379.6 49.8 %collective-permute-start = (bf16[128,8192]{1,0:T(8,128)(2,1)}, bf16[128,8192]{1,0:T(8,128)(2,1)}, u32[]{:S(2)}, u32[]{:S(2)}) collective-permute-start(bf16[128,8192]{1,0:T(8,128)(2,1)} %bitcast.25), channel_id=1, source_target_pairs={{32,0},{64,32},{96,64},{128,96},{160,128},{192,160},{224,192},{33,... | collective-permute-start | bytes 6291464 | tf_op jit(solution)/shard_map/ppermute | solution.py:14
  382.5 12.9 %all-to-all-start.5 = ((bf16[32,2,2048]{2,1,0:T(2,128)(2,1)}), bf16[32,2,2048]{2,1,0:T(2,128)(2,1)S(1)}, u32[]{:S(2)}, u32[]{:S(2)}) async-start(bf16[32,2,2048]{2,1,0:T(2,128)(2,1)} %reshape.198), calls=%async_computation.5 | async-start | bytes 524288 | tf_op jit(solution)/shard_map/all_to_all | solution.py:123
  395.4 20.8 %all-to-all-start.4 = ((bf16[256,32,64]{0,2,1:T(8,128)(2,1)}), bf16[256,32,64]{0,2,1:T(8,128)(2,1)S(1)}, u32[]{:S(2)}, u32[]{:S(2)}) async-start(bf16[256,32,64]{0,2,1:T(8,128)(2,1)} %fusion.12), calls=%async_computation.4 | async-start | bytes 2097152 | tf_op jit(solution)/shard_map/all_to_all | solution.py:122
Sparse Core Ops, SparseCore 0:
  10.6 111.3 all-gather.2
where the time goes:
time: 440 us; the launch traced here: 439 us
  blocking collectives  183 us (42%)
  local copies, waits for them, and re-layouts  110 us (25%)
  waiting for transfers between devices  74.8 us (17%)
  matrix products  29.6 us (7%)
  starting transfers between devices  26.9 us (6%)
  between operations  14.3 us (3%)
    psum x1, blocking collectives, local(): up_total, down_total = lax.psum((up_part, down_part), 'dp')  146 us
    gather x3, local copies, waits for them, and re-layouts, masked_rows(): picked = rows[row_index]  65.3 us
    all_to_all x1, blocking collectives, local(): lax.all_to_all(input_columns, 'dp', split_axis=0, concat_axis=1, tiled=True)  37 us
    all_to_all x1, waiting for transfers between devices, local(): lax.all_to_all(saved_rows, 'dp', split_axis=1, concat_axis=0, tiled=True)  25.3 us
    gather x1, local copies, waits for them, and re-layouts, adapter_term(): blocks.reshape(blocks.shape[0] * blocks.shape[1], blocks.shape[2])  19.5 us
    all_to_all x1, waiting for transfers between devices, local(): lax.all_to_all(down_grad_cols, 'dp', split_axis=1, concat_axis=0, tiled=T...  15.1 us
    all_gather x1, waiting for transfers between devices, local(): block_rows = lax.all_gather(grad_rows, 'dp', axis=0, tiled=True)  12.3 us
    dot_general x1, matrix products, local(): lax.dot_general(block_rows, weight, contract_last, preferred_element_type...  11.8 us
  transfers between devices with their start and end apart: 7, of which 6 were waited for; matrix products, arithmetic and copies ran while one was open for 14% of the time, Pallas kernels for 0%

commit v1 on v0

--- a/solution.py
+++ b/solution.py
@@ -2,6 +2,7 @@
 import jax.numpy as jnp
 from jax import lax
 from jax.sharding import PartitionSpec as P
+from jax.lax import all_to_all, axis_size
 
 ADAPTER_RANK = 64
 MOST = 256
@@ -67,7 +68,9 @@
     )
     saved_cols = lax.all_to_all(saved_rows, "dp", split_axis=1, concat_axis=0, tiled=True)
     saved_input_blocks = masked_rows(saved_cols, row_index, live_slot)
-    block_rows = lax.all_gather(grad_rows, "dp", axis=0, tiled=True)
+    block_rows = jnp.concatenate(
+        all_to_all(jnp.stack([grad_rows for _ in range(axis_size("dp"))]), "dp", 0, 0), axis=0
+    )
     frozen_part = lax.dot_general(
         block_rows, weight, contract_last, preferred_element_type=jnp.float32
     )

time: 440 us -> 663 us (1.51)
  waiting for transfers between devices: 74.8 us -> 241 us
  blocking collectives: 183 us -> 246 us
  between operations: 14.3 us -> 0.88 us
  local copies, waits for them, and re-layouts: 110 us -> 117 us
    all_to_all x1, waiting for transfers between devices: 25.3 us -> 191 us  [local(): all_to_all(jnp.stack([grad_rows for _ in range(axis_size('dp'))]), 'dp',...]
    all_to_all x0 -> x1, blocking collectives: none -> 32.1 us  [local(): lax.all_to_all(saved_rows, 'dp', split_axis=1, concat_axis=0, tiled=True)]
    psum x1, blocking collectives: 146 us -> 177 us  [local(): up_total, down_total = lax.psum((up_part, down_part), 'dp')]
    all_to_all x1, waiting for transfers between devices: 0.01 us -> 13.9 us  [local(): lax.all_to_all(adapter_down_maps[0], 'dp', split_axis=0, concat_axis=1, t...]
    all_gather x1 -> x0, waiting for transfers between devices: 12.3 us -> none  [local(): block_rows = lax.all_gather(grad_rows, 'dp', axis=0, tiled=True)]
    another operation x1 -> x2, local copies, waits for them, and re-layouts: 0.09 us -> 6.87 us  [the longest x1 6.78 us: local(): jnp.stack([grad_rows for _ in range(axis_size('dp'))])]
  transfers between devices with their start and end apart: 7 -> 6, of which waited for: 6 -> 6; matrix products, arithmetic and copies ran while one was open for 14% -> 8% of each run, Pallas kernels for 0% -> 0%
where the time goes in v1:
time: 663 us; the launch traced here: 662 us
  blocking collectives  246 us (37%)
  waiting for transfers between devices  241 us (36%)
  local copies, waits for them, and re-layouts  117 us (18%)
  matrix products  29.3 us (4%)
  starting transfers between devices  27.1 us (4%)
    all_to_all x1, waiting for transfers between devices, local(): all_to_all(jnp.stack([grad_rows for _ in range(axis_size('dp'))]), 'dp',...  191 us
    psum x1, blocking collectives, local(): up_total, down_total = lax.psum((up_part, down_part), 'dp')  177 us
    gather x3, local copies, waits for them, and re-layouts, masked_rows(): picked = rows[row_index]  65.1 us
    all_to_all x1, blocking collectives, local(): lax.all_to_all(input_columns, 'dp', split_axis=0, concat_axis=1, tiled=True)  37 us
    all_to_all x1, blocking collectives, local(): lax.all_to_all(saved_rows, 'dp', split_axis=1, concat_axis=0, tiled=True)  32.1 us
    gather x1, local copies, waits for them, and re-layouts, adapter_term(): blocks.reshape(blocks.shape[0] * blocks.shape[1], blocks.shape[2])  19.5 us
    all_to_all x1, waiting for transfers between devices, local(): lax.all_to_all(down_grad_cols, 'dp', split_axis=1, concat_axis=0, tiled=T...  15.1 us
    all_to_all x1, waiting for transfers between devices, local(): lax.all_to_all(adapter_down_maps[0], 'dp', split_axis=0, concat_axis=1, t...  13.9 us
  transfers between devices with their start and end apart: 6, of which 6 were waited for; matrix products, arithmetic and copies ran while one was open for 8% of the time, Pallas kernels for 0%

profile of v1, /device:TPU:1, one launch (start us, length us, event | category | flops | bytes accessed | tf_op | source)
XLA Modules:
  0.0 661.8 jit_solution(4481902951639756754)
XLA Ops:
  0.6 0.0 copy-start
  0.6 2.4 all_to_all.76
  3.0 0.0 copy-start.2
  3.0 2.2 copy.35
  5.2 2.1 reshape.199
  7.3 8.6 %all-to-all-start.1 = ((bf16[32,2,2048]{2,1,0:T(2,128)(2,1)}), bf16[32,2,2048]{2,1,0:T(2,128)(2,1)S(1)}, u32[]{:S(2)}, u32[]{:S(2)}) async-start(bf16[32,2,2048]{2,1,0:T(2,128)(2,1)} %reshape.199), calls=%async_computation.1 | async-start | bytes 524288 | tf_op jit(solution)/shard_map/all_to_all | solution.py:83
  15.9 1.5 copy.32
  17.4 1.6 copy.25
  19.0 5.9 all-to-all-done.1
  24.9 4.5 all-to-all-start.2
  29.4 0.0 copy-done.2
  29.4 0.6 copy.33
  30.0 2.5 copy.27
  32.5 13.9 %all-to-all-done.2 = bf16[32,256,64]{1,2,0:T(8,128)(2,1)} async-done(((bf16[32,256,64]{1,2,0:T(8,128)(2,1)}), bf16[32,256,64]{1,2,0:T(8,128)(2,1)}, u32[]{:S(2)}, u32[]{:S(2)}) %all-to-all-start.2) | async-done | bytes 1048608 | tf_op jit(solution)/shard_map/all_to_all | solution.py:82
  46.4 32.1 %all_to_all.101 = bf16[128,32,256]{2,0,1:T(8,128)(2,1)S(1)} all-to-all(bf16[128,32,256]{2,0,1:T(8,128)(2,1)} %copy.27), channel_id=1, replica_groups=mesh['section'=8,'dp'=32] {'dp'}, dimensions={1} | all-to-all | bytes 4194304 | tf_op jit(solution)/shard_map/all_to_all | solution.py:69
  78.5 6.8 %stack.3 = bf16[32,128,2048]{2,1,0:T(8,128)(2,1)} broadcast(bf16[128,2048]{1,0:T(8,128)(2,1)} %bitcast.86), dimensions={1,2} | broadcast | bytes 17301504 | tf_op jit(solution)/shard_map/stack | solution.py:72
  85.3 0.0 copy-start.4
  85.3 0.0 copy-start.5
  85.3 5.1 all-to-all-start
  90.4 0.0 copy-done.4
  90.4 0.2 convert_reduce_fusion
  90.6 0.1 copy.22
  90.6 0.1 reduce-window.7
  90.7 0.1 reduce
  90.8 0.0 copy-done.5
  90.8 0.1 select_reduce_fusion.3
  91.0 0.1 fusion.19
  91.1 0.2 select_reduce_fusion.1
  91.3 0.1 iota_compare_fusion.1
  91.4 1.2 reshape.200
  92.6 32.9 %gather_fusion.2 = bf16[8192,256]{1,0:T(8,128)(2,1)} fusion(bf16[4096,256]{1,0:T(8,128)(2,1)S(1)} %bitcast.73, s32[8192]{0:T(1024)S(1)} %broadcast_clamp_fusion), kind=kCustom, calls=%fused_computation.2 | custom fusion | bytes 8421376 | tf_op jit(solution)/shard_map/gather | solution.py:37
  125.5 4.3 fusion.1
  129.8 190.7 %all-to-all-done = bf16[32,128,2048]{2,1,0:T(8,128)(2,1)} async-done(((bf16[32,128,2048]{2,1,0:T(8,128)(2,1)}), bf16[32,128,2048]{2,1,0:T(8,128)(2,1)}, u32[]{:S(2)}, u32[]{:S(2)}) %all-to-all-start) | async-done | bytes 16777248 | tf_op jit(solution)/shard_map/all_to_all | solution.py:72
  320.5 1.6 constant_dynamic-slice_fusion
  322.1 29.5 %gather_fusion = bf16[8192,64]{1,0:T(8,128)(2,1)} fusion(bf16[4096,64]{1,0:T(8,128)(2,1)S(1)} %constant_dynamic-slice_fusion, s32[8192]{0:T(1024)S(1)} %broadcast_clamp_fusion), kind=kCustom, calls=%fused_computation | custom fusion | bytes 2129920 | tf_op jit(solution)/shard_map/gather | solution.py:37
  351.6 2.7 copy.23
  354.3 1.8 fusion.13
  356.1 177.0 %all-reduce.2 = (bf16[32,256,64]{1,2,0:T(8,128)(2,1)}, bf16[32,256,64]{1,2,0:T(8,128)(2,1)}) all-reduce(f32[32,256,64]{1,2,0:T(8,128)S(1)} %fusion.13, f32[32,256,64]{1,2,0:T(8,128)} %fusion.1), channel_id=1, replica_groups=mesh['section'=8,'dp'=32] {'dp'}, use_global_device_ids=true, to_apply=%region_4.5 | all-reduce | flops 1048576 | bytes 6291456 | tf_op jit(solution)/shard_map/psum | solution.py:94
  533.1 6.1 fusion.9
  539.1 19.5 %gather_fusion.1 = f32[4096,256]{1,0:T(8,128)} fusion(f32[8192,256]{1,0:T(8,128)} %bitcast.74, s32[4096]{0:T(1024)S(1)} %broadcast_clamp_fusion.1), kind=kCustom, calls=%fused_computation.1 | custom fusion | bytes 8404992 | tf_op jit(solution)/shard_map/gather | solution.py:45
  558.6 0.0 copy-done
  558.6 11.8 %fusion = bf16[4096,256]{1,0:T(8,128)(2,1)S(1)} fusion(bf16[4096,2048]{1,0:T(8,128)(2,1)} %bitcast.1, f32[4096,256]{1,0:T(8,128)} %gather_fusion.1, bf16[1,256,2048]{2,1,0:T(8,128)(2,1)S(1)} %copy-done), kind=kOutput, calls=%fused_computation.4 | convolution fusion | flops 4298113024 | bytes 24117248 | tf_op jit(solution)/shard_map/dot_general | solution.py:74
  570.5 0.0 copy-start.1
  570.5 0.0 copy-start.6
  570.5 37.0 %all_to_all.102 = bf16[32,128,256]{2,1,0:T(8,128)(2,1)S(1)} all-to-all(bf16[32,128,256]{2,1,0:T(8,128)(2,1)S(1)} %bitcast.83), channel_id=1, replica_groups=mesh['section'=8,'dp'=32] {'dp'}, dimensions={0} | all-to-all | bytes 4194304 | tf_op jit(solution)/shard_map/all_to_all | solution.py:129
  607.5 1.5 copy.30
  609.0 1.3 collective-permute-start
  610.3 0.0 copy-done.1
  610.3 0.0 copy-done.6
  610.3 0.4 fusion.24
  610.8 1.1 reshape.201
  611.9 3.9 all-to-all-start.6
  615.9 0.0 copy-done.3
  615.9 4.8 fusion.5
  620.7 4.2 all-to-all-done.6
  624.8 3.8 all-to-all-start.5
  628.6 0.4 reshape.202
  629.0 0.3 copy.29
  629.4 1.2 broadcast_in_dim.53
  630.5 15.1 %all-to-all-done.5 = bf16[256,32,64]{0,2,1:T(8,128)(2,1)S(1)} async-done(((bf16[256,32,64]{0,2,1:T(8,128)(2,1)}), bf16[256,32,64]{0,2,1:T(8,128)(2,1)S(1)}, u32[]{:S(2)}, u32[]{:S(2)}) %all-to-all-start.5) | async-done | bytes 1048608 | tf_op jit(solution)/shard_map/all_to_all | solution.py:125
  645.6 0.6 copy.28
  646.2 1.3 broadcast_in_dim.52
  647.5 11.2 %collective-permute-done = bf16[128,8192]{1,0:T(8,128)(2,1)} collective-permute-done((bf16[128,8192]{1,0:T(8,128)(2,1)}, bf16[128,8192]{1,0:T(8,128)(2,1)}, u32[]{:S(2)}, u32[]{:S(2)}) %collective-permute-start) | collective-permute-done | bytes 2097184 | tf_op jit(solution)/shard_map/ppermute | solution.py:15
  658.7 3.1 copy.41
  (8 shorter events, 0.1 us)
Async XLA Ops:
  0.6 558.0 %copy-start = (bf16[1,256,2048]{2,1,0:T(8,128)(2,1)S(1)}, bf16[1,256,2048]{2,1,0:T(8,128)(2,1)}, u32[]{:S(2)}) copy-start(bf16[1,256,2048]{2,1,0:T(8,128)(2,1)} %param.9) | copy-start | bytes 3145732
  3.0 26.4 %copy-start.2 = (bf16[1,128,8192]{2,1,0:T(8,128)(2,1)S(1)}, bf16[1,128,8192]{2,1,0:T(8,128)(2,1)}, u32[]{:S(2)}) copy-start(bf16[1,128,8192]{2,1,0:T(8,128)(2,1)} %param.8) | copy-start | bytes 6291460
  7.3 17.6 %all-to-all-start.1 = ((bf16[32,2,2048]{2,1,0:T(2,128)(2,1)}), bf16[32,2,2048]{2,1,0:T(2,128)(2,1)S(1)}, u32[]{:S(2)}, u32[]{:S(2)}) async-start(bf16[32,2,2048]{2,1,0:T(2,128)(2,1)} %reshape.199), calls=%async_computation.1 | async-start | bytes 524288 | tf_op jit(solution)/shard_map/all_to_all | solution.py:83
  24.9 21.5 %all-to-all-start.2 = ((bf16[32,256,64]{1,2,0:T(8,128)(2,1)}), bf16[32,256,64]{1,2,0:T(8,128)(2,1)}, u32[]{:S(2)}, u32[]{:S(2)}) async-start(bf16[32,256,64]{1,2,0:T(8,128)(2,1)} %copy.25), calls=%async_computation.2 | async-start | bytes 2097152 | tf_op jit(solution)/shard_map/all_to_all | solution.py:82
  85.3 5.1 copy-start.4
  85.3 5.6 copy-start.5
  85.3 235.2 %all-to-all-start = ((bf16[32,128,2048]{2,1,0:T(8,128)(2,1)}), bf16[32,128,2048]{2,1,0:T(8,128)(2,1)}, u32[]{:S(2)}, u32[]{:S(2)}) async-start(bf16[32,128,2048]{2,1,0:T(8,128)(2,1)} %stack.3), calls=%async_computation | async-start | bytes 33554432 | tf_op jit(solution)/shard_map/all_to_all | solution.py:72
  570.5 39.9 %copy-start.1 = (bf16[32,256,64]{1,2,0:T(8,128)(2,1)S(1)}, bf16[32,256,64]{1,2,0:T(8,128)(2,1)}, u32[]{:S(2)}) copy-start(bf16[32,256,64]{1,2,0:T(8,128)(2,1)} %copy.23) | copy-start | bytes 3145732
  570.5 39.9 %copy-start.6 = (bf16[32,256,64]{1,2,0:T(8,128)(2,1)S(1)}, bf16[32,256,64]{1,2,0:T(8,128)(2,1)}, u32[]{:S(2)}) copy-start(bf16[32,256,64]{1,2,0:T(8,128)(2,1)} %get-tuple-element.8) | copy-start | bytes 3145732
  607.5 8.3 %copy-start.3 = (bf16[32,256,64]{1,2,0:T(8,128)(2,1)S(1)}, bf16[32,256,64]{1,2,0:T(8,128)(2,1)}, u32[]{:S(2)}) copy-start(bf16[32,256,64]{1,2,0:T(8,128)(2,1)} %get-tuple-element.7) | copy-start | bytes 3145732
  609.0 49.7 %collective-permute-start = (bf16[128,8192]{1,0:T(8,128)(2,1)}, bf16[128,8192]{1,0:T(8,128)(2,1)}, u32[]{:S(2)}, u32[]{:S(2)}) collective-permute-start(bf16[128,8192]{1,0:T(8,128)(2,1)} %bitcast.25), channel_id=1, source_target_pairs={{32,0},{64,32},{96,64},{128,96},{160,128},{192,160},{224,192},{33,... | collective-permute-start | bytes 6291464 | tf_op jit(solution)/shard_map/ppermute | solution.py:15
  611.9 12.9 %all-to-all-start.6 = ((bf16[32,2,2048]{2,1,0:T(2,128)(2,1)}), bf16[32,2,2048]{2,1,0:T(2,128)(2,1)S(1)}, u32[]{:S(2)}, u32[]{:S(2)}) async-start(bf16[32,2,2048]{2,1,0:T(2,128)(2,1)} %reshape.201), calls=%async_computation.6 | async-start | bytes 524288 | tf_op jit(solution)/shard_map/all_to_all | solution.py:126
  624.8 20.8 %all-to-all-start.5 = ((bf16[256,32,64]{0,2,1:T(8,128)(2,1)}), bf16[256,32,64]{0,2,1:T(8,128)(2,1)S(1)}, u32[]{:S(2)}, u32[]{:S(2)}) async-start(bf16[256,32,64]{0,2,1:T(8,128)(2,1)} %fusion.5), calls=%async_computation.5 | async-start | bytes 2097152 | tf_op jit(solution)/shard_map/all_to_all | solution.py:125
